TPU v7x, 32 devices: a whole 2x2x4 slice. The times are simulated.
32 devices in a mesh: groups: 2 (over y), blk: 4 (over z), head: 4 (over x, core).
Axes of the slice: x: 2, y: 2, z: 4, core: 2. Of those that a mesh axis runs over, the one named last changes fastest.
Arguments:
- queries: bfloat16 [4096, 4096], P(('groups', 'blk', 'head')), parts along dimension 0, may hold values from -8 to 8
- keys: bfloat16 [4096, 4096], P(('groups', 'blk', 'head')), parts along dimension 0, may hold values from -8 to 8
- values: bfloat16 [4096, 4096], P(('groups', 'blk', 'head')), parts along dimension 0, may hold values from -6 to 6
- scale_qk: float32 [4096], replicated, may hold values from 0.7 to 8
- w_out: bfloat16 [4096, 4096], P('head'), may hold values from -0.09375 to 0.09375
- stretch_start: int32 [32], P(('groups', 'blk', 'head')), parts along dimension 0, may hold values from 0 to 1920, as said below
Outputs:
- attended: bfloat16 [4096, 4096], P(('groups', 'blk', 'head')), parts along dimension 0
There are 2 independent parts, one for each index of `groups`. A program takes and returns all parts, laid end to end along the dimension named above; an argument that names none is the same for every part. Nothing has to cross between parts.
Inputs may be any that keep to these rules, and one draw needn't show every extreme that they name: stretch_start[b * 4 + h] = (((b + r) % 4) * 4 + h) * 128 for an offset r of 0 to 3 drawn from the seed.
All inputs are finite; a program needn't handle non-finite values.
Results may differ from a plain program's by a relative error of at most 0.04.
Values may be sent and summed in bfloat16 or wider, within the bound.
A program may use at most 128 MiB of HBM per device.

v0:
```python
import jax
import jax.numpy as jnp
from jax import lax
from jax.sharding import PartitionSpec as P

H = 32
DH = 128
WSEG = 2


def shifted(value, axis, steps):
    count = lax.axis_size(axis)
    pairs = [(source, (source + steps) % count) for source in range(count)]
    return lax.ppermute(value, axis, pairs)


def shortened(array):

    def short(part):
        return part.astype(jnp.bfloat16) if part.dtype == jnp.float32 else part

    return jax.tree.map(short, array)


def normalize(rows, scale_qk):
    x = rows.astype(jnp.float32).reshape(rows.shape[0], H, DH)
    x = x * lax.rsqrt(jnp.mean(x * x, axis=2, keepdims=True) + 1e-06)
    return (x.reshape(rows.shape[0], H * DH) * scale_qk[None, :]).astype(jnp.bfloat16)


def attend(state, q_block, q_pos, k_block, v_block, k_pos, reach):
    partial_out, running_max, running_total = state
    heads = running_max.shape[0]
    q_rows = q_block.shape[0]
    k_rows = k_block.shape[0]
    q_three = q_block.reshape(q_rows, heads, DH)
    k_three = k_block.reshape(k_rows, heads, DH)
    v_three = v_block.reshape(k_rows, heads, DH)
    scores = jnp.einsum("qhd,khd->hqk", q_three, k_three, preferred_element_type=jnp.float32) * (
        1.0 / DH**0.5
    )
    allowed = ((q_pos[:, None] >= k_pos[None, :]) & (q_pos[:, None] - k_pos[None, :] < reach))[
        None, :, :
    ]
    peak = jnp.max(jnp.where(allowed, scores, -1e30), axis=2)
    new_max = jnp.maximum(running_max, peak)
    weights = jnp.where(allowed, jnp.exp(scores - new_max[:, :, None]), jnp.float32(0.0))
    fade = jnp.exp(running_max - new_max)
    new_total = running_total * fade + jnp.sum(weights, axis=2)
    mixed = jnp.einsum(
        "hqk,khd->qhd", weights.astype(jnp.bfloat16), v_three, preferred_element_type=jnp.float32
    )
    updated = partial_out.reshape(q_rows, heads, DH) * jnp.transpose(fade)[:, :, None] + mixed
    return (updated.reshape(q_rows, heads * DH), new_max, new_total)


def visit(state, q_block, q_pos, k_block, v_block, k_pos, reach):
    return attend(state, q_block, q_pos, k_block, v_block, k_pos, reach)


def shards(queries, keys, values, scale_qk, w_out, stretch_start):
    tok_rows = queries.shape[0]
    q_norm = normalize(queries, scale_qk)
    k_norm = normalize(keys, scale_qk)
    q_seg, k_seg, v_seg = (
        lax.all_to_all(q_norm, "head", split_axis=1, concat_axis=0, tiled=True),
        lax.all_to_all(k_norm, "head", split_axis=1, concat_axis=0, tiled=True),
        lax.all_to_all(values, "head", split_axis=1, concat_axis=0, tiled=True),
    )
    seg_rows = q_seg.shape[0]
    heads = q_seg.shape[1] // DH
    whole_len = lax.axis_size("blk") * seg_rows
    reach = WSEG * seg_rows
    seg_first = stretch_start[0] - lax.axis_index("head") * tok_rows
    inner = jnp.arange(seg_rows, dtype=jnp.int32)
    my_pos = seg_first + inner
    state = (
        jnp.zeros((seg_rows, heads * DH), jnp.float32),
        jnp.full((heads, seg_rows), -1e30, jnp.float32),
        jnp.zeros((heads, seg_rows), jnp.float32),
    )
    q_block = q_seg
    for step in range(WSEG + 1):
        first = seg_first + step * seg_rows
        q_pos = (
            jnp.where(
                first >= whole_len,
                first - whole_len,
                jnp.where(first < 0, first + whole_len, first),
            )
            + inner
        )
        state = visit(state, q_block, q_pos, k_seg, v_seg, my_pos, reach)
        if step < WSEG:
            q_block = shifted(q_block, "blk", -1)
            state = shifted(
                (shortened(state[0]), shortened(state[1]), shortened(state[2])), "blk", -1
            )
    partial_out, running_total = shifted((shortened(state[0]), shortened(state[2])), "blk", WSEG)
    scaled = partial_out.reshape(seg_rows, heads, DH) / jnp.transpose(running_total)[:, :, None]
    heads_out = scaled.reshape(seg_rows, heads * DH).astype(jnp.bfloat16)
    return lax.psum_scatter(
        jnp.dot(heads_out, w_out, preferred_element_type=jnp.float32).astype(jnp.bfloat16),
        "head",
        scatter_dimension=0,
        tiled=True,
    )


def solution(mesh):
    return jax.shard_map(
        shards,
        mesh=mesh,
        in_specs=(
            P(("groups", "blk", "head"), None),
            P(("groups", "blk", "head"), None),
            P(("groups", "blk", "head"), None),
            P(),
            P("head", None),
            P(("groups", "blk", "head")),
        ),
        out_specs=P(("groups", "blk", "head"), None),
        check_vma=False,
    )
```

profile of v0, /device:TPU:0, one launch (start us, length us, event | category | flops | bytes accessed | tf_op | source)
XLA Modules:
  0.0 275.9 jit_solution(9354994491467485652)
XLA Ops:
  6.5 2.3 copy.47
  8.8 4.2 %all-to-all-start.2 = ((bf16[128,4,1024]{0,2,1:T(8,128)(2,1)}), bf16[128,4,1024]{0,2,1:T(8,128)(2,1)S(1)}, u32[]{:S(2)}, u32[]{:S(2)}) async-start(bf16[128,4,1024]{0,2,1:T(8,128)(2,1)} %bitcast.10), calls=%async_computation.2 | async-start | bytes 2097152 | tf_op jit(solution)/shard_map/all_to_all | solution.py:68
  13.0 1.6 copy.43
  14.6 1.6 copy.41
  16.3 0.2 bitcast_reduce_fusion
  16.5 0.2 bitcast_reduce_fusion.1
  16.8 0.0 copy-done.5
  16.8 1.7 fusion.27
  18.5 1.5 copy.44
  20.0 7.5 %all-to-all-done.2 = bf16[128,4,1024]{0,2,1:T(8,128)(2,1)S(1)} async-done(((bf16[128,4,1024]{0,2,1:T(8,128)(2,1)}), bf16[128,4,1024]{0,2,1:T(8,128)(2,1)S(1)}, u32[]{:S(2)}, u32[]{:S(2)}) %all-to-all-start.2) | async-done | bytes 1048608 | tf_op jit(solution)/shard_map/all_to_all | solution.py:68
  27.5 16.9 %all_to_all.51 = bf16[128,4,1024]{2,0,1:T(8,128)(2,1)S(1)} all-to-all(bf16[128,4,1024]{2,0,1:T(8,128)(2,1)S(1)} %copy.44), channel_id=1, replica_groups=mesh['groups'=2,'blk'=4,'head'=4] {'head'}, dimensions={1} | all-to-all | bytes 2097152 | tf_op jit(solution)/shard_map/all_to_all | solution.py:67
  44.4 3.5 %all-to-all-start = ((bf16[128,4,1024]{0,2,1:T(8,128)(2,1)}), bf16[128,4,1024]{0,2,1:T(8,128)(2,1)S(1)}, u32[]{:S(2)}, u32[]{:S(2)}) async-start(bf16[128,4,1024]{0,2,1:T(8,128)(2,1)} %bitcast.66), calls=%async_computation | async-start | bytes 2097152 | tf_op jit(solution)/shard_map/all_to_all | solution.py:66
  47.9 0.0 reduce-scatter.2.cloned.1.call-start
  48.6 1.6 fusion.39
  50.2 1.8 copy.48
  52.0 2.2 reshape.270
  54.2 0.3 copy.65
  54.5 7.8 %all-to-all-done = bf16[128,4,1024]{0,2,1:T(8,128)(2,1)S(1)} async-done(((bf16[128,4,1024]{0,2,1:T(8,128)(2,1)}), bf16[128,4,1024]{0,2,1:T(8,128)(2,1)S(1)}, u32[]{:S(2)}, u32[]{:S(2)}) %all-to-all-start) | async-done | bytes 1048608 | tf_op jit(solution)/shard_map/all_to_all | solution.py:66
  62.3 0.5 copy.42
  62.8 0.0 copy-start.1
  62.8 0.3 copy.64
  63.1 0.0 copy-start.2
  63.1 2.9 %select_reduce_fusion.2 = (f32[8,512]{1,0:T(8,128)S(1)}, f32[8,512,512]{1,2,0:T(8,128)S(1)}) fusion(pred[512,512]{0,1:T(8,128)(4,1)} %get-tuple-element.16, bf16[512,8,128]{2,1,0:T(8,128)(2,1)S(1)} %bitcast.58, bf16[512,8,128]{2,1,0:T(8,128)(2,1)S(1)} %bitcast.70), kind=kOutput, calls=%fused_computation.5 | convolution fusion | flops 543158272 | bytes 10764288 | tf_op jit(solution)/shard_map/qhd,khd->hqk/dot_general | solution.py:39
  66.0 4.4 %collective-permute-start.2 = (bf16[512,1024]{1,0:T(8,128)(2,1)S(1)}, bf16[512,1024]{1,0:T(8,128)(2,1)}, u32[]{:S(2)}, u32[]{:S(2)}) collective-permute-start(bf16[512,1024]{1,0:T(8,128)(2,1)S(1)} %bitcast.65), channel_id=1, source_target_pairs={{0,12},{4,0},{8,4},{12,8},{1,13},{5,1},{9,5},{13,9},{2,14},{6,2},{... | collective-permute-start | bytes 3145736 | tf_op jit(solution)/shard_map/ppermute | solution.py:14
  70.4 0.0 copy-done.1
  70.4 1.7 fusion
  72.2 0.0 copy-start
  72.2 3.0 %fusion.32 = bf16[512,8,128]{0,2,1:T(8,128)(2,1)} fusion(bf16[512,8,128]{0,2,1:T(8,128)(2,1)S(1)} %copy-done.2, f32[8,512,512]{1,2,0:T(8,128)S(1)} %get-tuple-element.19, f32[8,512]{1,0:T(8,128)S(1)} %broadcast_maximum_fusion, pred[512,512]{0,1:T(8,128)(4,1)S(1)} %copy-done.1, f32[512,8]{0,1:T(8,128)S(1)} %get-tuple-element.12), kind=kOutput, calls=%fused_computation.43 | convolution fusion | flops 546308096 | bytes 10780672 | tf_op jit(solution)/shard_map/hqk,khd->qhd/dot_general | solution.py:50
  75.3 0.4 collective-permute-start
  75.7 0.4 collective-permute-start.1
  76.2 0.1 collective-permute-start.7
  76.3 17.8 %collective-permute-done.2 = bf16[512,1024]{1,0:T(8,128)(2,1)} collective-permute-done((bf16[512,1024]{1,0:T(8,128)(2,1)S(1)}, bf16[512,1024]{1,0:T(8,128)(2,1)}, u32[]{:S(2)}, u32[]{:S(2)}) %collective-permute-start.2) | collective-permute-done | bytes 1048608 | tf_op jit(solution)/shard_map/ppermute | solution.py:14
  94.0 1.5 copy.51
  95.5 0.0 copy-done
  95.5 0.0 copy-start.3
  95.5 1.6 select_reduce_fusion.1
  97.2 18.2 %collective-permute-done.1 = bf16[8,512]{1,0:T(8,128)(2,1)S(1)} collective-permute-done((bf16[8,512]{1,0:T(8,128)(2,1)S(1)}, bf16[8,512]{1,0:T(8,128)(2,1)S(1)}, u32[]{:S(2)}, u32[]{:S(2)}) %collective-permute-start.1) | collective-permute-done | bytes 8224 | tf_op jit(solution)/shard_map/ppermute | solution.py:14
  115.4 1.7 fusion.2
  117.1 4.3 %collective-permute-start.5 = (bf16[512,1024]{1,0:T(8,128)(2,1)}, bf16[512,1024]{1,0:T(8,128)(2,1)}, u32[]{:S(2)}, u32[]{:S(2)}) collective-permute-start(bf16[512,1024]{1,0:T(8,128)(2,1)} %collective-permute-done.2), channel_id=1, source_target_pairs={{0,12},{4,0},{8,4},{12,8},{1,13},{5,1},{9,5},{13,9},{2,14},{6,2},{... | collective-permute-start | bytes 3145736 | tf_op jit(solution)/shard_map/ppermute | solution.py:14
  121.5 0.0 collective-permute-done.7
  121.5 2.1 fusion.8
  123.6 0.0 collective-permute-done
  123.6 2.6 fusion.31
  126.1 0.0 collective-permute-start.3
  126.2 0.0 collective-permute-start.4
  126.2 0.6 collective-permute-start.8
  126.8 18.6 %collective-permute-done.5 = bf16[512,1024]{1,0:T(8,128)(2,1)} collective-permute-done((bf16[512,1024]{1,0:T(8,128)(2,1)}, bf16[512,1024]{1,0:T(8,128)(2,1)}, u32[]{:S(2)}, u32[]{:S(2)}) %collective-permute-start.5) | collective-permute-done | bytes 1048608 | tf_op jit(solution)/shard_map/ppermute | solution.py:14
  145.4 1.5 copy.55
  146.9 1.6 select_reduce_fusion
  148.6 17.2 %collective-permute-done.4 = bf16[8,512]{1,0:T(8,128)(2,1)S(1)} collective-permute-done((bf16[8,512]{1,0:T(8,128)(2,1)S(1)}, bf16[8,512]{1,0:T(8,128)(2,1)S(1)}, u32[]{:S(2)}, u32[]{:S(2)}) %collective-permute-start.4) | collective-permute-done | bytes 8224 | tf_op jit(solution)/shard_map/ppermute | solution.py:14
  165.8 1.7 fusion.4
  167.5 0.0 collective-permute-done.8
  167.5 0.0 slice-start.1
  167.6 2.1 fusion.6
  169.6 0.0 collective-permute-done.3
  169.7 1.6 fusion.29
  171.2 1.4 collective-permute-start.6
  172.6 1.6 collective-permute-start.9
  174.2 43.6 %collective-permute-done.9 = bf16[8,512]{1,0:T(8,128)(2,1)S(1)} collective-permute-done((bf16[8,512]{1,0:T(8,128)(2,1)S(1)}, bf16[8,512]{1,0:T(8,128)(2,1)S(1)}, u32[]{:S(2)}, u32[]{:S(2)}) %collective-permute-start.9) | collective-permute-done | bytes 8224 | tf_op jit(solution)/shard_map/ppermute | solution.py:14
  217.8 0.0 collective-permute-done.6
  217.8 0.1 bitcast_divide_fusion
  217.9 6.4 %convolution_convert_fusion = bf16[512,4096]{1,0:T(8,128)(2,1)} fusion(bf16[512,1024]{0,1:T(8,128)(2,1)S(1)} %bitcast_divide_fusion, bf16[1024,4096]{1,0:T(8,128)(2,1)S(1)} %bitcast.74), kind=kOutput, calls=%fused_computation.12 | convolution fusion | flops 4297064448 | bytes 13631488 | tf_op jit(solution)/shard_map/dot_general | solution.py:103
  224.3 0.0 reduce-scatter.2.cloned.1.call-update
  224.4 44.7 %reduce-scatter.2.cloned.1.call-done = bf16[128,4096]{1,0:T(8,128)(2,1)} async-done(((bf16[512,4096]{1,0:T(8,128)(2,1)}), bf16[128,4096]{1,0:T(8,128)(2,1)}) %reduce-scatter.2.cloned.1.call-update) | async-done | bytes 1048592 | tf_op jit(solution)/shard_map/reduce_scatter | solution.py:102
  (19 shorter events, 0.1 us)
Async XLA Ops:
  6.5 10.2 %copy-start.5 = (f32[4096]{0:T(1024)S(1)}, f32[4096]{0:T(1024)}, u32[]{:S(2)}) copy-start(f32[4096]{0:T(1024)} %param.9) | copy-start | bytes 49156
  8.8 18.7 %all-to-all-start.2 = ((bf16[128,4,1024]{0,2,1:T(8,128)(2,1)}), bf16[128,4,1024]{0,2,1:T(8,128)(2,1)S(1)}, u32[]{:S(2)}, u32[]{:S(2)}) async-start(bf16[128,4,1024]{0,2,1:T(8,128)(2,1)} %bitcast.10), calls=%async_computation.2 | async-start | bytes 2097152 | tf_op jit(solution)/shard_map/all_to_all | solution.py:68
  44.4 18.0 %all-to-all-start = ((bf16[128,4,1024]{0,2,1:T(8,128)(2,1)}), bf16[128,4,1024]{0,2,1:T(8,128)(2,1)S(1)}, u32[]{:S(2)}, u32[]{:S(2)}) async-start(bf16[128,4,1024]{0,2,1:T(8,128)(2,1)} %bitcast.66), calls=%async_computation | async-start | bytes 2097152 | tf_op jit(solution)/shard_map/all_to_all | solution.py:66
  47.9 221.2 %reduce-scatter.2.cloned.1.call-start = ((), (), s32[]{:S(2)}) async-start(), calls=%async_computation.4 | async-start | bytes 5242880 | tf_op jit(solution)/shard_map/reduce_scatter | solution.py:102
  62.8 7.6 %copy-start.1 = (pred[512,512]{0,1:T(8,128)(4,1)S(1)}, pred[512,512]{0,1:T(8,128)(4,1)}, u32[]{:S(2)}) copy-start(pred[512,512]{0,1:T(8,128)(4,1)} %get-tuple-element.16) | copy-start | bytes 786436
  63.1 9.1 %copy-start.2 = (bf16[512,8,128]{0,2,1:T(8,128)(2,1)S(1)}, bf16[512,8,128]{0,2,1:T(8,128)(2,1)}, u32[]{:S(2)}) copy-start(bf16[512,8,128]{0,2,1:T(8,128)(2,1)} %reshape.270) | copy-start | bytes 3145732
  66.0 28.0 %collective-permute-start.2 = (bf16[512,1024]{1,0:T(8,128)(2,1)S(1)}, bf16[512,1024]{1,0:T(8,128)(2,1)}, u32[]{:S(2)}, u32[]{:S(2)}) collective-permute-start(bf16[512,1024]{1,0:T(8,128)(2,1)S(1)} %bitcast.65), channel_id=1, source_target_pairs={{0,12},{4,0},{8,4},{12,8},{1,13},{5,1},{9,5},{13,9},{2,14},{6,2},{... | collective-permute-start | bytes 3145736 | tf_op jit(solution)/shard_map/ppermute | solution.py:14
  72.2 23.4 %copy-start = (pred[512,512]{0,1:T(8,128)(4,1)S(1)}, pred[512,512]{0,1:T(8,128)(4,1)}, u32[]{:S(2)}) copy-start(pred[512,512]{0,1:T(8,128)(4,1)} %get-tuple-element.17) | copy-start | bytes 786436
  75.3 48.3 %collective-permute-start = (bf16[512,1024]{0,1:T(8,128)(2,1)}, bf16[512,1024]{0,1:T(8,128)(2,1)}, u32[]{:S(2)}, u32[]{:S(2)}) collective-permute-start(bf16[512,1024]{0,1:T(8,128)(2,1)} %bitcast.13), channel_id=1, source_target_pairs={{0,12},{4,0},{8,4},{12,8},{1,13},{5,1},{9,5},{13,9},{2,14},{6,2},{... | collective-permute-start | bytes 3145736 | tf_op jit(solution)/shard_map/ppermute | solution.py:14
  75.7 39.7 %collective-permute-start.1 = (bf16[8,512]{1,0:T(8,128)(2,1)S(1)}, bf16[8,512]{1,0:T(8,128)(2,1)S(1)}, u32[]{:S(2)}, u32[]{:S(2)}) collective-permute-start(bf16[8,512]{1,0:T(8,128)(2,1)S(1)} %fusion.56), channel_id=1, source_target_pairs={{0,12},{4,0},{8,4},{12,8},{1,13},{5,1},{9,5},{13,9},{2,14},{6,2},{... | collective-permute-start | bytes 24584 | tf_op jit(solution)/shard_map/ppermute | solution.py:14
  76.2 45.3 %collective-permute-start.7 = (bf16[8,512]{1,0:T(8,128)(2,1)S(1)}, bf16[8,512]{1,0:T(8,128)(2,1)S(1)}, u32[]{:S(2)}, u32[]{:S(2)}) collective-permute-start(bf16[8,512]{1,0:T(8,128)(2,1)S(1)} %get-tuple-element.11), channel_id=1, source_target_pairs={{0,12},{4,0},{8,4},{12,8},{1,13},{5,1},{9,5},{13,9},{2,14},{6,2},{... | collective-permute-start | bytes 24584 | tf_op jit(solution)/shard_map/ppermute | solution.py:14
  95.5 26.0 %copy-start.3 = (bf16[512,8,128]{0,2,1:T(8,128)(2,1)S(1)}, bf16[512,8,128]{0,2,1:T(8,128)(2,1)}, u32[]{:S(2)}) copy-start(bf16[512,8,128]{0,2,1:T(8,128)(2,1)} %reshape.270) | copy-start | bytes 3145732
  117.1 28.3 %collective-permute-start.5 = (bf16[512,1024]{1,0:T(8,128)(2,1)}, bf16[512,1024]{1,0:T(8,128)(2,1)}, u32[]{:S(2)}, u32[]{:S(2)}) collective-permute-start(bf16[512,1024]{1,0:T(8,128)(2,1)} %collective-permute-done.2), channel_id=1, source_target_pairs={{0,12},{4,0},{8,4},{12,8},{1,13},{5,1},{9,5},{13,9},{2,14},{6,2},{... | collective-permute-start | bytes 3145736 | tf_op jit(solution)/shard_map/ppermute | solution.py:14
  126.1 43.5 %collective-permute-start.3 = (bf16[512,1024]{0,1:T(8,128)(2,1)}, bf16[512,1024]{0,1:T(8,128)(2,1)}, u32[]{:S(2)}, u32[]{:S(2)}) collective-permute-start(bf16[512,1024]{0,1:T(8,128)(2,1)} %bitcast.19), channel_id=1, source_target_pairs={{0,12},{4,0},{8,4},{12,8},{1,13},{5,1},{9,5},{13,9},{2,14},{6,2},{... | collective-permute-start | bytes 3145736 | tf_op jit(solution)/shard_map/ppermute | solution.py:14
  126.2 39.6 %collective-permute-start.4 = (bf16[8,512]{1,0:T(8,128)(2,1)S(1)}, bf16[8,512]{1,0:T(8,128)(2,1)S(1)}, u32[]{:S(2)}, u32[]{:S(2)}) collective-permute-start(bf16[8,512]{1,0:T(8,128)(2,1)S(1)} %get-tuple-element.5), channel_id=1, source_target_pairs={{0,12},{4,0},{8,4},{12,8},{1,13},{5,1},{9,5},{13,9},{2,14},{6,2},{... | collective-permute-start | bytes 24584 | tf_op jit(solution)/shard_map/ppermute | solution.py:14
  126.2 41.3 %collective-permute-start.8 = (bf16[8,512]{1,0:T(8,128)(2,1)S(1)}, bf16[8,512]{1,0:T(8,128)(2,1)S(1)}, u32[]{:S(2)}, u32[]{:S(2)}) collective-permute-start(bf16[8,512]{1,0:T(8,128)(2,1)S(1)} %get-tuple-element.9), channel_id=1, source_target_pairs={{0,12},{4,0},{8,4},{12,8},{1,13},{5,1},{9,5},{13,9},{2,14},{6,2},{... | collective-permute-start | bytes 24584 | tf_op jit(solution)/shard_map/ppermute | solution.py:14
  146.9 20.6 %copy-start.4 = (bf16[512,8,128]{0,2,1:T(8,128)(2,1)S(1)}, bf16[512,8,128]{0,2,1:T(8,128)(2,1)}, u32[]{:S(2)}) copy-start(bf16[512,8,128]{0,2,1:T(8,128)(2,1)} %reshape.270) | copy-start | bytes 3145732
  165.8 52.1 %slice-start = ((s8[8388608]{0:T(1024)(128)(4,1)}), s8[4194304]{0:T(1024)(128)(4,1)S(1)}, s32[]{:S(2)}) async-start(s8[8388608]{0:T(1024)(128)(4,1)} %bitcast.73), calls=%async_computation.5 | async-start | bytes 8388608
  167.5 50.4 %slice-start.1 = ((s8[8388608]{0:T(1024)(128)(4,1)}), s8[4194304]{0:T(1024)(128)(4,1)S(1)}, s32[]{:S(2)}) async-start(s8[8388608]{0:T(1024)(128)(4,1)} %bitcast.73), calls=%async_computation.6 | async-start | bytes 8388608
  171.2 46.6 %collective-permute-start.6 = (bf16[512,1024]{0,1:T(8,128)(2,1)S(1)}, bf16[512,1024]{0,1:T(8,128)(2,1)S(1)}, u32[]{:S(2)}, u32[]{:S(2)}) collective-permute-start(bf16[512,1024]{0,1:T(8,128)(2,1)S(1)} %bitcast.71), channel_id=1, source_target_pairs={{0,8},{4,12},{8,0},{12,4},{1,9},{5,13},{9,1},{13,5},{2,10},{6,14},... | collective-permute-start | bytes 3145736 | tf_op jit(solution)/shard_map/ppermute | solution.py:14
  172.6 45.2 %collective-permute-start.9 = (bf16[8,512]{1,0:T(8,128)(2,1)S(1)}, bf16[8,512]{1,0:T(8,128)(2,1)S(1)}, u32[]{:S(2)}, u32[]{:S(2)}) collective-permute-start(bf16[8,512]{1,0:T(8,128)(2,1)S(1)} %get-tuple-element.7), channel_id=1, source_target_pairs={{0,8},{4,12},{8,0},{12,4},{1,9},{5,13},{9,1},{13,5},{2,10},{6,14},... | collective-permute-start | bytes 24584 | tf_op jit(solution)/shard_map/ppermute | solution.py:14
Sparse Core Ops, SparseCore 0:
  224.5 44.5 reduce-scatter.1
where the time goes:
time: 276 us
  waiting for transfers between devices  175 us (63%)
  starting transfers between devices  21.2 us (8%)
  matrix products  19.7 us (7%)
  blocking collectives  16.9 us (6%)
  local copies, waits for them, and re-layouts  15.1 us (5%)
  between operations  14.4 us (5%)
  other arithmetic  13.3 us (5%)
    ppermute x10, waiting for transfers between devices, shifted(): return lax.ppermute(value, axis, pairs)  115 us
    reduce_scatter x1, waiting for transfers between devices, shards(): lax.psum_scatter(jnp.dot(heads_out, w_out, preferred_element_type=jnp.flo...  44.7 us
    all_to_all x1, blocking collectives, shards(): lax.all_to_all(k_norm, 'head', split_axis=1, concat_axis=0, tiled=True)  16.9 us
    ppermute x10, starting transfers between devices, shifted(): return lax.ppermute(value, axis, pairs)  13.4 us
    all_to_all x1, waiting for transfers between devices, shards(): lax.all_to_all(q_norm, 'head', split_axis=1, concat_axis=0, tiled=True)  7.79 us
    all_to_all x1, waiting for transfers between devices, shards(): lax.all_to_all(values, 'head', split_axis=1, concat_axis=0, tiled=True)  7.51 us
    dot_general x3, matrix products, attend(): jnp.einsum('hqk,khd->qhd', weights.astype(jnp.bfloat16), v_three, preferr...  7.19 us
    dot_general x1, matrix products, shards(): jnp.dot(heads_out, w_out, preferred_element_type=jnp.float32)  6.4 us
  transfers between devices with their start and end apart: 13, of which 8 were waited for; matrix products, arithmetic and copies ran while one was open for 12% of the time, Pallas kernels for 0%

commit v1 on v0

v1 whole, which is shorter than its diff:
```python
import functools

import jax
import jax.numpy as jnp
from jax import lax
from jax.experimental import pallas as pl
from jax.experimental.pallas import tpu as pltpu
from jax.sharding import PartitionSpec as P

DH = 128
SCORE = 1.4426950408889634 / DH**0.5
NC = 2


def kernel(
    nh, nb, q_hbm, k_hbm, v_hbm, scale_ref, w_hbm, start_ref, out_ref,
    qin, kin, qn, kn, w_ref, qseg, kbuf, vbuf, ho, sib_out, sib_in, comb, rbuf,
    load_sem, loc_sem, a2a_s, a2a_r, h1_s, h1_r, h2_s, h2_r, sib_s, sib_r, red_s, red_r,
):
    t, hd = qin.shape
    cols = hd // nh
    heads = cols // DH
    seg = nh * t
    win = 2 * seg + t
    width = w_ref.shape[1]
    half = width // 2
    chunk = half // NC
    nx = nh // 2
    me = lax.axis_index("head")
    z = lax.axis_index("blk")
    chip = me // 2
    core = me % 2
    sib = chip * 2 + (1 - core)
    nxt = (z + 1) % nb
    prv = (z + nb - 1) % nb

    def partner(jx, jc):
        return ((chip + jx) % nx) * 2 + (core + jc) % 2

    others = [(jx, 0) for jx in range(1, nx)] + [(jx, 1) for jx in range(nx)]
    arrival = [(jx, jc) for jx in range(nx) for jc in range(2) if jx or jc]

    loads = [
        pltpu.make_async_copy(k_hbm, kin, load_sem.at[0]),
        pltpu.make_async_copy(q_hbm, qin, load_sem.at[1]),
        pltpu.make_async_copy(w_hbm, w_ref, load_sem.at[2]),
    ]
    for copy in loads:
        copy.start()

    barrier = pltpu.get_barrier_semaphore()
    for jx, jc in others:
        pl.semaphore_signal(barrier, inc=1, device_id={"head": partner(jx, jc)})
    pl.semaphore_signal(barrier, inc=1, device_id={"blk": nxt})
    pl.semaphore_signal(barrier, inc=1, device_id={"blk": prv})
    pl.semaphore_wait(barrier, nh + 1)

    def group(ref, peer):
        return ref.at[:, pl.ds(pl.multiple_of(peer * cols, DH), cols)]

    def piece(ref, base, index):
        return ref.at[pl.ds(pl.multiple_of(base + index * t, t), t), :]

    def swap(kind, src, dst, base, peer, source):
        return pltpu.make_async_remote_copy(
            src_ref=group(src, peer), dst_ref=piece(dst, base, source),
            send_sem=a2a_s.at[kind, peer], recv_sem=a2a_r.at[kind, source],
            device_id={"head": peer},
        )

    def hop(src, dst, kind, base, index, send, recv):
        return pltpu.make_async_remote_copy(
            src_ref=src, dst_ref=piece(dst, base, index),
            send_sem=send.at[kind, index], recv_sem=recv.at[kind, index],
            device_id={"blk": nxt},
        )

    def normed(src, dst, peer):
        for h in range(heads):
            at = pl.ds(pl.multiple_of(peer * cols + h * DH, DH), DH)
            x = src[:, at].astype(jnp.float32)
            x = x * lax.rsqrt(jnp.mean(x * x, axis=1, keepdims=True) + 1e-06)
            dst[:, at] = (x * scale_ref[:, at]).astype(jnp.bfloat16)

    hop(group(v_hbm, me), vbuf, 1, seg, me, h1_s, h1_r).start()
    for jx, jc in others:
        swap(1, v_hbm, vbuf, 2 * seg, partner(jx, jc), me).start()
    own_v = pltpu.make_async_copy(group(v_hbm, me), piece(vbuf, 2 * seg, me), loc_sem.at[1])
    own_v.start()

    loads[0].wait()
    normed(kin, kn, me)
    hop(group(kn, me), kbuf, 0, seg, me, h1_s, h1_r).start()
    own_k = pltpu.make_async_copy(group(kn, me), piece(kbuf, 2 * seg, me), loc_sem.at[0])
    own_k.start()
    for jx, jc in others:
        peer = partner(jx, jc)
        normed(kin, kn, peer)
        swap(0, kn, kbuf, 2 * seg, peer, me).start()

    loads[1].wait()
    for jx, jc in others:
        peer = partner(jx, jc)
        normed(qin, qn, peer)
        swap(2, qn, qseg, 0, peer, me).start()
    normed(qin, qn, me)
    own_q = pltpu.make_async_copy(group(qn, me), piece(qseg, 0, me), loc_sem.at[2])
    own_q.start()

    for jx, jc in arrival:
        source = partner(jx, jc)
        swap(1, v_hbm, vbuf, 2 * seg, source, source).wait_recv()
        hop(piece(vbuf, 2 * seg, source), vbuf, 1, seg, source, h1_s, h1_r).start()
        swap(0, kn, kbuf, 2 * seg, source, source).wait_recv()
        hop(piece(kbuf, 2 * seg, source), kbuf, 0, seg, source, h1_s, h1_r).start()

    def relay(step, carry):
        i = nh - 1 - step
        for kind, buf in ((0, kbuf), (1, vbuf)):
            hop(piece(buf, 2 * seg, i), buf, kind, seg, i, h1_s, h1_r).wait_recv()
            hop(piece(buf, seg, i), buf, kind, 0, i, h2_s, h2_r).start()
        return carry

    lax.fori_loop(0, nh, relay, 0)
    for jx, jc in arrival:
        source = partner(jx, jc)
        swap(2, qn, qseg, 0, source, source).wait_recv()
    own_q.wait()
    own_k.wait()
    own_v.wait()
    loads[2].wait()

    first = start_ref[0] - me * t
    row = lax.broadcasted_iota(jnp.int32, (t, win), 0)
    col = lax.broadcasted_iota(jnp.int32, (t, win), 1)

    def to_sibling(i, c):
        at = pl.ds(c * chunk, chunk)
        return pltpu.make_async_remote_copy(
            src_ref=sib_out.at[i, :, at], dst_ref=sib_in.at[i, :, at],
            send_sem=sib_s.at[i, c], recv_sem=sib_r.at[i, c],
            device_id={"head": sib},
        )

    def to_owner(i, c, source, owner):
        at = pl.ds(c * chunk, chunk)
        return pltpu.make_async_remote_copy(
            src_ref=comb.at[i, :, at], dst_ref=rbuf.at[source, :, at],
            send_sem=red_s.at[i, c], recv_sem=red_r.at[source, c],
            device_id={"head": owner},
        )

    def block(step, carry):
        i = nh - 1 - step
        for kind, buf in ((0, kbuf), (1, vbuf)):
            hop(piece(buf, seg, i), buf, kind, 0, i, h2_s, h2_r).wait_recv()
        rows = pl.ds(pl.multiple_of(i * t, t), t)
        keys = pl.ds(pl.multiple_of(i * t, t), win)
        allowed = (col > row) & (col <= row + 2 * seg) & (col >= 2 * seg - first - i * t)
        for h in range(heads):
            at = pl.ds(h * DH, DH)
            s = lax.dot_general(
                qseg[rows, at], kbuf[keys, at], (((1,), (1,)), ((), ())),
                preferred_element_type=jnp.float32,
            )
            s = jnp.where(allowed, s, -1e30)
            p = jnp.exp2((s - jnp.max(s, axis=1, keepdims=True)) * SCORE)
            total = jnp.sum(p, axis=1, keepdims=True)
            o = jnp.dot(p.astype(jnp.bfloat16), vbuf[keys, at], preferred_element_type=jnp.float32)
            ho[:, at] = (o / total).astype(jnp.bfloat16)

        def project(side, c):
            at = pl.ds(pl.multiple_of(side * half + c * chunk, DH), chunk)
            return jnp.dot(ho[...], w_ref[:, at], preferred_element_type=jnp.float32)

        for c in range(NC):
            sib_out[i, :, pl.ds(c * chunk, chunk)] = project(1 - core, c).astype(jnp.bfloat16)
            to_sibling(i, c).start()
        for c in range(NC):
            at = pl.ds(c * chunk, chunk)
            mine = project(core, c)
            to_sibling(i, c).wait_recv()
            both = (mine + sib_in[i, :, at].astype(jnp.float32)).astype(jnp.bfloat16)

            @pl.when(me == i)
            def _():
                rbuf[me, :, at] = both

            @pl.when(me != i)
            def _():
                comb[i, :, at] = both
                to_owner(i, c, me, i).start()

        return carry

    lax.fori_loop(0, nh, block, 0)

    for c in range(NC):
        at = pl.ds(c * chunk, chunk)
        for jx, jc in arrival:
            source = partner(jx, jc)
            to_owner(source, c, source, source).wait_recv()
        for side in range(2):
            total = rbuf[side, :, at].astype(jnp.float32)
            for x in range(1, nx):
                total = total + rbuf[2 * x + side, :, at].astype(jnp.float32)
            out_ref[:, pl.ds(side * half + c * chunk, chunk)] = total.astype(jnp.bfloat16)

    for jx, jc in arrival:
        peer = partner(jx, jc)
        swap(1, v_hbm, vbuf, 2 * seg, peer, me).wait_send()
        swap(0, kn, kbuf, 2 * seg, peer, me).wait_send()
        swap(2, qn, qseg, 0, peer, me).wait_send()
        for c in range(NC):
            to_owner(peer, c, me, peer).wait_send()

    def sent(i, carry):
        for kind, buf in ((0, kbuf), (1, vbuf)):
            hop(piece(buf, 2 * seg, i), buf, kind, seg, i, h1_s, h1_r).wait_send()
            hop(piece(buf, seg, i), buf, kind, 0, i, h2_s, h2_r).wait_send()
        for c in range(NC):
            to_sibling(i, c).wait_send()
        return carry

    lax.fori_loop(0, nh, sent, 0)


def solution(mesh):
    nh = mesh.shape["head"]
    nb = mesh.shape["blk"]

    def shards(queries, keys, values, scale_qk, w_out, stretch_start):
        t, hd = queries.shape
        cols = hd // nh
        seg = nh * t
        width = w_out.shape[1]
        half = width // 2
        bf16 = jnp.bfloat16
        dma = pltpu.SemaphoreType.DMA
        anywhere = pl.BlockSpec(memory_space=pl.ANY)
        vmem = pl.BlockSpec(memory_space=pltpu.VMEM)
        return pl.pallas_call(
            functools.partial(kernel, nh, nb),
            out_shape=jax.ShapeDtypeStruct((t, width), bf16),
            in_specs=[anywhere, anywhere, anywhere, vmem, anywhere,
                      pl.BlockSpec(memory_space=pltpu.SMEM)],
            out_specs=vmem,
            scratch_shapes=[
                pltpu.VMEM((t, hd), bf16),
                pltpu.VMEM((t, hd), bf16),
                pltpu.VMEM((t, hd), bf16),
                pltpu.VMEM((t, hd), bf16),
                pltpu.VMEM((cols, width), bf16),
                pltpu.VMEM((seg, cols), bf16),
                pltpu.VMEM((3 * seg, cols), bf16),
                pltpu.VMEM((3 * seg, cols), bf16),
                pltpu.VMEM((t, cols), bf16),
                pltpu.VMEM((nh, t, half), bf16),
                pltpu.VMEM((nh, t, half), bf16),
                pltpu.VMEM((nh, t, half), bf16),
                pltpu.VMEM((nh, t, half), bf16),
                dma((3,)),
                dma((3,)),
                dma((3, nh)),
                dma((3, nh)),
                dma((2, nh)),
                dma((2, nh)),
                dma((2, nh)),
                dma((2, nh)),
                dma((nh, NC)),
                dma((nh, NC)),
                dma((nh, NC)),
                dma((nh, NC)),
            ],
            compiler_params=pltpu.CompilerParams(
                collective_id=0, has_side_effects=True, vmem_limit_bytes=56 * 1024 * 1024
            ),
        )(queries, keys, values, scale_qk.reshape(1, hd), w_out, stretch_start)

    return jax.shard_map(
        shards,
        mesh=mesh,
        in_specs=(
            P(("groups", "blk", "head"), None),
            P(("groups", "blk", "head"), None),
            P(("groups", "blk", "head"), None),
            P(),
            P("head", None),
            P(("groups", "blk", "head")),
        ),
        out_specs=P(("groups", "blk", "head"), None),
        check_vma=False,
    )
```

time: 276 us -> 122 us (0.44)
  waiting for transfers between devices: 175 us -> 0 us
  Pallas kernels: 0 us -> 119 us
  starting transfers between devices: 21.2 us -> 0 us
  matrix products: 19.7 us -> 0 us
  blocking collectives: 16.9 us -> 0 us
  between operations: 14.4 us -> 0.66 us
  other arithmetic: 13.3 us -> 0 us
  local copies, waits for them, and re-layouts: 15.1 us -> 2.29 us
    pallas_call x0 -> x1, Pallas kernels: none -> 119 us  [shards(): pl.pallas_call(functools.partial(kernel, nh, nb), out_shape=jax.ShapeDtyp...]
    ppermute x10 -> x0, waiting for transfers between devices: 115 us -> none  [shifted(): return lax.ppermute(value, axis, pairs)]
    reduce_scatter x1 -> x0, waiting for transfers between devices: 44.7 us -> none  [shards(): lax.psum_scatter(jnp.dot(heads_out, w_out, preferred_element_type=jnp.flo...]
    dot_general x7 -> x0, matrix products: 19.7 us -> none  [the longest x3 7.19 us: attend(): jnp.einsum('hqk,khd->qhd', weights.astype(jnp.bfloat16), v_three, preferr...]
    all_to_all x1 -> x0, blocking collectives: 16.9 us -> none  [shards(): lax.all_to_all(k_norm, 'head', split_axis=1, concat_axis=0, tiled=True)]
    all_to_all x2 -> x0, waiting for transfers between devices: 15.3 us -> none  [the longest x1 7.79 us: shards(): lax.all_to_all(q_norm, 'head', split_axis=1, concat_axis=0, tiled=True)]
    ppermute x10 -> x0, starting transfers between devices: 13.4 us -> none  [shifted(): return lax.ppermute(value, axis, pairs)]
    all_to_all x2 -> x0, starting transfers between devices: 7.72 us -> none  [the longest x1 4.21 us: shards(): lax.all_to_all(values, 'head', split_axis=1, concat_axis=0, tiled=True)]
  transfers between devices with their start and end apart: 13 -> 0, of which waited for: 8 -> 0; matrix products, arithmetic and copies ran while one was open for 12% -> 0% of each run, Pallas kernels for 0% -> 0%
where the time goes in v1:
time: 122 us
  Pallas kernels  119 us (98%)
  local copies, waits for them, and re-layouts  2.29 us (2%)
    pallas_call x1, Pallas kernels, shards(): pl.pallas_call(functools.partial(kernel, nh, nb), out_shape=jax.ShapeDtyp...  119 us

profile of v1, /device:TPU:0, one launch (start us, length us, event | category | flops | bytes accessed | tf_op | source)
XLA Modules:
  0.0 121.9 jit_solution(3612519416583716754)
XLA Ops:
  0.7 119.0 %shard_map.64 = bf16[128,4096]{1,0:T(8,128)(2,1)} custom-call(bf16[128,4096]{1,0:T(8,128)(2,1)} %q_hbm.1, bf16[128,4096]{1,0:T(8,128)(2,1)} %k_hbm.1, bf16[128,4096]{1,0:T(8,128)(2,1)} %v_hbm.1, f32[1,4096]{1,0:T(1,128)} %bitcast.1, bf16[1024,4096]{1,0:T(8,128)(2,1)} %w_hbm.1, s32[1]{0:T(128)S(6)} %copy.8.start_ref), custom_call_target="tpu_custom_call" | custom-call | tf_op jit(solution)/shard_map/pallas_call | solution.py:242
  119.7 2.3 %copy.9 = bf16[128,4096]{1,0:T(8,128)(2,1)} copy(bf16[128,4096]{1,0:T(8,128)(2,1)} %shard_map.64) | data formatting | bytes 2097152

commit v2 on v1

v2 whole, which is shorter than its diff:
```python
import functools

import jax
import jax.numpy as jnp
from jax import lax
from jax.experimental import pallas as pl
from jax.experimental.pallas import tpu as pltpu
from jax.sharding import PartitionSpec as P

DH = 128
SCORE = 1.4426950408889634 / DH**0.5
NC = 2
NS = 2


def kernel(
    nh, nb, q_hbm, k_hbm, v_hbm, scale_ref, w_hbm, start_ref, rbuf,
    qin, kin, qn, kn, w_ref, qseg, kbuf, vbuf, acc, ho, sib_out, sib_in, comb,
    load_sem, loc_sem, keep_sem, a2a_s, a2a_r, h1_s, h1_r, h2_s, h2_r, sib_s, sib_r, red_s, red_r,
):
    t, hd = qin.shape
    cols = hd // nh
    heads = cols // DH
    seg = nh * t
    sub = t // NS
    width = w_ref.shape[1]
    half = width // 2
    chunk = half // NC
    nx = nh // 2
    me = lax.axis_index("head")
    z = lax.axis_index("blk")
    chip = me // 2
    core = me % 2
    sib = chip * 2 + (1 - core)
    nxt = (z + 1) % nb
    prv = (z + nb - 1) % nb

    def partner(jx, jc):
        return ((chip + jx) % nx) * 2 + (core + jc) % 2

    others = [(jx, 0) for jx in range(1, nx)] + [(jx, 1) for jx in range(nx)]
    arrival = [(jx, jc) for jx in range(nx) for jc in range(2) if jx or jc]

    loads = [
        pltpu.make_async_copy(k_hbm, kin, load_sem.at[0]),
        pltpu.make_async_copy(q_hbm, qin, load_sem.at[1]),
        pltpu.make_async_copy(w_hbm, w_ref, load_sem.at[2]),
    ]
    for copy in loads:
        copy.start()

    barrier = pltpu.get_barrier_semaphore()
    for jx, jc in others:
        pl.semaphore_signal(barrier, inc=1, device_id={"head": partner(jx, jc)})
    pl.semaphore_signal(barrier, inc=1, device_id={"blk": nxt})
    pl.semaphore_signal(barrier, inc=1, device_id={"blk": prv})
    pl.semaphore_wait(barrier, nh + 1)

    def group(ref, peer):
        return ref.at[:, pl.ds(pl.multiple_of(peer * cols, DH), cols)]

    def piece(ref, base, index):
        return ref.at[pl.ds(pl.multiple_of(base + index * t, t), t), :]

    def swap(kind, src, dst, base, peer, source):
        return pltpu.make_async_remote_copy(
            src_ref=group(src, peer), dst_ref=piece(dst, base, source),
            send_sem=a2a_s.at[kind, peer], recv_sem=a2a_r.at[kind, source],
            device_id={"head": peer},
        )

    def hop(src, dst, kind, base, index, send, recv):
        return pltpu.make_async_remote_copy(
            src_ref=src, dst_ref=piece(dst, base, index),
            send_sem=send.at[kind, index], recv_sem=recv.at[kind, index],
            device_id={"blk": nxt},
        )

    def normed(src, dst, peer):
        for h in range(heads):
            at = pl.ds(pl.multiple_of(peer * cols + h * DH, DH), DH)
            x = src[:, at].astype(jnp.float32)
            x = x * lax.rsqrt(jnp.mean(x * x, axis=1, keepdims=True) + 1e-06)
            dst[:, at] = (x * scale_ref[:, at]).astype(jnp.bfloat16)

    hop(group(v_hbm, me), vbuf, 1, seg, me, h1_s, h1_r).start()
    for jx, jc in others:
        swap(1, v_hbm, vbuf, 2 * seg, partner(jx, jc), me).start()
    own_v = pltpu.make_async_copy(group(v_hbm, me), piece(vbuf, 2 * seg, me), loc_sem.at[1])
    own_v.start()

    loads[0].wait()
    normed(kin, kn, me)
    hop(group(kn, me), kbuf, 0, seg, me, h1_s, h1_r).start()
    own_k = pltpu.make_async_copy(group(kn, me), piece(kbuf, 2 * seg, me), loc_sem.at[0])
    own_k.start()
    for jx, jc in others:
        peer = partner(jx, jc)
        normed(kin, kn, peer)
        swap(0, kn, kbuf, 2 * seg, peer, me).start()

    loads[1].wait()
    for jx, jc in [(0, 0)] + others:
        normed(qin, qn, partner(jx, jc))
    own_q = pltpu.make_async_copy(group(qn, me), piece(qseg, 0, me), loc_sem.at[2])
    own_q.start()

    def onward(kind, src, buf, jx, jc):
        source = partner(jx, jc)
        swap(kind, src, buf, 2 * seg, source, source).wait_recv()
        hop(piece(buf, 2 * seg, source), buf, kind, seg, source, h1_s, h1_r).start()

    onward(1, v_hbm, vbuf, 0, 1)
    onward(0, kn, kbuf, 0, 1)
    for jx, jc in arrival[1:]:
        onward(1, v_hbm, vbuf, jx, jc)
    for jx, jc in arrival[1:]:
        onward(0, kn, kbuf, jx, jc)
    for jx, jc in others:
        peer = partner(jx, jc)
        swap(2, qn, qseg, 0, peer, me).start()

    def slab(ref, base, i, part):
        return ref.at[pl.ds(pl.multiple_of(base + i * t + part * sub, sub), sub), :]

    def pass_on(kind, buf, i, part):
        return pltpu.make_async_remote_copy(
            src_ref=slab(buf, seg, i, part), dst_ref=slab(buf, 0, i, part),
            send_sem=h2_s.at[kind, i, part], recv_sem=h2_r.at[kind, i, part],
            device_id={"blk": nxt},
        )

    def relay(step, carry):
        i = nh - 1 - step
        for kind, buf in ((0, kbuf), (1, vbuf)):
            hop(piece(buf, 2 * seg, i), buf, kind, seg, i, h1_s, h1_r).wait_recv()
        for part in reversed(range(NS)):
            for kind, buf in ((0, kbuf), (1, vbuf)):
                pass_on(kind, buf, i, part).start()
        return carry

    lax.fori_loop(0, nh, relay, 0)
    for jx, jc in arrival:
        source = partner(jx, jc)
        swap(2, qn, qseg, 0, source, source).wait_recv()
    own_q.wait()
    own_k.wait()
    own_v.wait()
    loads[2].wait()

    first = start_ref[0] - me * t
    row = lax.broadcasted_iota(jnp.int32, (t, 2 * seg), 0)
    col = lax.broadcasted_iota(jnp.int32, (t, 2 * seg), 1)

    def to_sibling(i, part, c):
        at = (i, pl.ds(part * sub, sub), pl.ds(c * chunk, chunk))
        return pltpu.make_async_remote_copy(
            src_ref=sib_out.at[at], dst_ref=sib_in.at[at],
            send_sem=sib_s.at[i, part, c], recv_sem=sib_r.at[i, part, c],
            device_id={"head": sib},
        )

    def home(x, side, part, c):
        columns = pl.ds(pl.multiple_of(side * half + c * chunk, DH), chunk)
        return rbuf.at[x, pl.ds(part * sub, sub), columns]

    def to_owner(i, part, c, source, owner):
        return pltpu.make_async_remote_copy(
            src_ref=comb.at[i, pl.ds(part * sub, sub), pl.ds(c * chunk, chunk)],
            dst_ref=home(source // 2, source % 2, part, c),
            send_sem=red_s.at[i, part, c], recv_sem=red_r.at[source, part, c],
            device_id={"head": owner},
        )

    def keep(i, part, c):
        return pltpu.make_async_copy(
            comb.at[i, pl.ds(part * sub, sub), pl.ds(c * chunk, chunk)],
            home(chip, core, part, c), keep_sem.at[part, c],
        )

    def block(step, carry):
        i = nh - 1 - step
        rows = pl.ds(pl.multiple_of(i * t, t), t)
        keys = pl.ds(pl.multiple_of(i * t + t, t), 2 * seg)
        oldest = 2 * seg - first - i * t
        allowed = (col <= row + (2 * seg - t)) & (col >= oldest - t)
        held = []
        for h in range(heads):
            at = pl.ds(h * DH, DH)
            s = lax.dot_general(
                qseg[rows, at], kbuf[keys, at], (((1,), (1,)), ((), ())),
                preferred_element_type=jnp.float32,
            )
            s = jnp.where(allowed, s, -1e30)
            peak = jnp.max(s, axis=1, keepdims=True)
            p = jnp.exp2((s - peak) * SCORE)
            held.append((peak, jnp.sum(p, axis=1, keepdims=True)))
            acc[:, at] = jnp.dot(
                p.astype(jnp.bfloat16), vbuf[keys, at], preferred_element_type=jnp.float32
            )

        for part in reversed(range(NS)):
            for kind, buf in ((0, kbuf), (1, vbuf)):
                pass_on(kind, buf, i, part).wait_recv()
            low = part * sub
            many = t - low
            keys = pl.ds(pl.multiple_of(i * t + low, sub), many)
            here = pl.ds(pl.multiple_of(i * t + low, sub), sub)
            age = lax.broadcasted_iota(jnp.int32, (sub, many), 1)
            allowed = (age > lax.broadcasted_iota(jnp.int32, (sub, many), 0)) & (
                age >= oldest - low
            )
            for h in range(heads):
                at = pl.ds(h * DH, DH)
                s = lax.dot_general(
                    qseg[here, at], kbuf[keys, at], (((1,), (1,)), ((), ())),
                    preferred_element_type=jnp.float32,
                )
                s = jnp.where(allowed, s, -1e30)
                peak, total = (value[low:low + sub] for value in held[h])
                top = jnp.maximum(peak, jnp.max(s, axis=1, keepdims=True))
                p = jnp.exp2((s - top) * SCORE)
                fade = jnp.exp2((peak - top) * SCORE)
                total = total * fade + jnp.sum(p, axis=1, keepdims=True)
                o = acc[pl.ds(low, sub), at] * fade + jnp.dot(
                    p.astype(jnp.bfloat16), vbuf[keys, at], preferred_element_type=jnp.float32
                )
                ho[pl.ds(low, sub), at] = (o / total).astype(jnp.bfloat16)

            spot = pl.ds(low, sub)

            def project(side, c):
                at = pl.ds(pl.multiple_of(side * half + c * chunk, DH), chunk)
                return jnp.dot(ho[spot, :], w_ref[:, at], preferred_element_type=jnp.float32)

            for c in range(NC):
                sib_out[i, spot, pl.ds(c * chunk, chunk)] = project(1 - core, c).astype(
                    jnp.bfloat16
                )
                to_sibling(i, part, c).start()
            for c in range(NC):
                at = pl.ds(c * chunk, chunk)
                mine = project(core, c)
                to_sibling(i, part, c).wait_recv()
                both = mine + sib_in[i, spot, at].astype(jnp.float32)
                comb[i, spot, at] = both.astype(jnp.bfloat16)

                @pl.when(me == i)
                def _():
                    keep(i, part, c).start()

                @pl.when(me != i)
                def _():
                    to_owner(i, part, c, me, i).start()

        return carry

    lax.fori_loop(0, nh, block, 0)

    pieces = [(part, c) for part in reversed(range(NS)) for c in range(NC)]
    for part, c in pieces:
        keep(me, part, c).wait()
        for jx, jc in arrival:
            source = partner(jx, jc)
            to_owner(source, part, c, source, source).wait_recv()

    for jx, jc in arrival:
        peer = partner(jx, jc)
        swap(1, v_hbm, vbuf, 2 * seg, peer, me).wait_send()
        swap(0, kn, kbuf, 2 * seg, peer, me).wait_send()
        swap(2, qn, qseg, 0, peer, me).wait_send()
        for part, c in pieces:
            to_owner(peer, part, c, me, peer).wait_send()

    def sent(i, carry):
        for kind, buf in ((0, kbuf), (1, vbuf)):
            hop(piece(buf, 2 * seg, i), buf, kind, seg, i, h1_s, h1_r).wait_send()
            for part in range(NS):
                pass_on(kind, buf, i, part).wait_send()
        for part, c in pieces:
            to_sibling(i, part, c).wait_send()
        return carry

    lax.fori_loop(0, nh, sent, 0)


def solution(mesh):
    nh = mesh.shape["head"]
    nb = mesh.shape["blk"]

    def shards(queries, keys, values, scale_qk, w_out, stretch_start):
        t, hd = queries.shape
        cols = hd // nh
        seg = nh * t
        width = w_out.shape[1]
        half = width // 2
        bf16 = jnp.bfloat16
        dma = pltpu.SemaphoreType.DMA
        anywhere = pl.BlockSpec(memory_space=pl.ANY)
        vmem = pl.BlockSpec(memory_space=pltpu.VMEM)
        parts = pl.pallas_call(
            functools.partial(kernel, nh, nb),
            out_shape=jax.ShapeDtypeStruct((nh // 2, t, width), bf16),
            in_specs=[anywhere, anywhere, anywhere, vmem, anywhere,
                      pl.BlockSpec(memory_space=pltpu.SMEM)],
            out_specs=anywhere,
            scratch_shapes=[
                pltpu.VMEM((t, hd), bf16),
                pltpu.VMEM((t, hd), bf16),
                pltpu.VMEM((t, hd), bf16),
                pltpu.VMEM((t, hd), bf16),
                pltpu.VMEM((cols, width), bf16),
                pltpu.VMEM((seg, cols), bf16),
                pltpu.VMEM((3 * seg, cols), bf16),
                pltpu.VMEM((3 * seg, cols), bf16),
                pltpu.VMEM((t, cols), jnp.float32),
                pltpu.VMEM((t, cols), bf16),
                pltpu.VMEM((nh, t, half), bf16),
                pltpu.VMEM((nh, t, half), bf16),
                pltpu.VMEM((nh, t, half), bf16),
                dma((3,)),
                dma((3,)),
                dma((NS, NC)),
                dma((3, nh)),
                dma((3, nh)),
                dma((2, nh)),
                dma((2, nh)),
                dma((2, nh, NS)),
                dma((2, nh, NS)),
                dma((nh, NS, NC)),
                dma((nh, NS, NC)),
                dma((nh, NS, NC)),
                dma((nh, NS, NC)),
            ],
            compiler_params=pltpu.CompilerParams(
                collective_id=0, has_side_effects=True, vmem_limit_bytes=56 * 1024 * 1024
            ),
        )(queries, keys, values, scale_qk.reshape(1, hd), w_out, stretch_start)
        return jnp.sum(parts.astype(jnp.float32), axis=0).astype(bf16)

    return jax.shard_map(
        shards,
        mesh=mesh,
        in_specs=(
            P(("groups", "blk", "head"), None),
            P(("groups", "blk", "head"), None),
            P(("groups", "blk", "head"), None),
            P(),
            P("head", None),
            P(("groups", "blk", "head")),
        ),
        out_specs=P(("groups", "blk", "head"), None),
        check_vma=False,
    )
```

time: 122 us -> 118 us (0.967)
  Pallas kernels: 119 us -> 114 us
  other arithmetic: 0 us -> 3.26 us
  local copies, waits for them, and re-layouts: 2.29 us -> 0 us
    pallas_call x1, Pallas kernels: 119 us -> 114 us  [shards(): pl.pallas_call(functools.partial(kernel, nh, nb), out_shape=jax.ShapeDtyp...]
    reduce_sum x0 -> x1, other arithmetic: none -> 3.26 us  [shards(): return jnp.sum(parts.astype(jnp.float32), axis=0).astype(bf16)]
    unnamed x1 -> x0, local copies, waits for them, and re-layouts: 2.29 us -> none
where the time goes in v2:
time: 118 us
  Pallas kernels  114 us (97%)
  other arithmetic  3.26 us (3%)
    pallas_call x1, Pallas kernels, shards(): pl.pallas_call(functools.partial(kernel, nh, nb), out_shape=jax.ShapeDtyp...  114 us
    reduce_sum x1, other arithmetic, shards(): return jnp.sum(parts.astype(jnp.float32), axis=0).astype(bf16)  3.26 us

profile of v2, /device:TPU:0, one launch (start us, length us, event | category | flops | bytes accessed | tf_op | source)
XLA Modules:
  0.0 117.7 jit_solution(12605595506582191656)
XLA Ops:
  0.7 113.7 %shard_map.64 = bf16[2,128,4096]{2,1,0:T(8,128)(2,1)} custom-call(bf16[128,4096]{1,0:T(8,128)(2,1)} %q_hbm.1, bf16[128,4096]{1,0:T(8,128)(2,1)} %k_hbm.1, bf16[128,4096]{1,0:T(8,128)(2,1)} %v_hbm.1, f32[1,4096]{1,0:T(1,128)} %bitcast.1, bf16[1024,4096]{1,0:T(8,128)(2,1)} %w_hbm.1, s32[1]{0:T(128)S(6)} %copy.7.start_ref), custom_call_target="tpu_custom_call" | custom-call | tf_op jit(solution)/shard_map/pallas_call | solution.py:301
  114.4 3.3 %reduce_sum.12 = bf16[128,4096]{1,0:T(8,128)(2,1)} reduce(bf16[2,128,4096]{2,1,0:T(8,128)(2,1)} %shard_map.64, bf16[]{:T(256)} %constant.2.clone.1), dimensions={0}, to_apply=%region_0.0 | reduce | flops 524288 | bytes 3145730 | tf_op jit(solution)/shard_map/reduce_sum | solution.py:339

commit v3 on v2

--- a/solution.py
+++ b/solution.py
@@ -10,7 +10,7 @@
 DH = 128
 SCORE = 1.4426950408889634 / DH**0.5
 NC = 2
-NS = 2
+SLOTS = 3
 
 
 def kernel(
@@ -22,7 +22,8 @@
     cols = hd // nh
     heads = cols // DH
     seg = nh * t
-    sub = t // NS
+    usual = ((0, t // 2, t // 2), (1, 0, t // 2))
+    final = ((0, t // 2, t // 2), (1, t // 4, t // 4), (2, 0, t // 4))
     width = w_ref.shape[1]
     half = width // 2
     chunk = half // NC
@@ -120,26 +121,50 @@
         peer = partner(jx, jc)
         swap(2, qn, qseg, 0, peer, me).start()
 
-    def slab(ref, base, i, part):
-        return ref.at[pl.ds(pl.multiple_of(base + i * t + part * sub, sub), sub), :]
+    def slab(ref, base, i, low, size):
+        return ref.at[pl.ds(pl.multiple_of(base + i * t + low, size), size), :]
 
     def pass_on(kind, buf, i, part):
+        slot, low, size = part
         return pltpu.make_async_remote_copy(
-            src_ref=slab(buf, seg, i, part), dst_ref=slab(buf, 0, i, part),
-            send_sem=h2_s.at[kind, i, part], recv_sem=h2_r.at[kind, i, part],
+            src_ref=slab(buf, seg, i, low, size), dst_ref=slab(buf, 0, i, low, size),
+            send_sem=h2_s.at[kind, i, slot], recv_sem=h2_r.at[kind, i, slot],
             device_id={"blk": nxt},
         )
 
-    def relay(step, carry):
-        i = nh - 1 - step
-        for kind, buf in ((0, kbuf), (1, vbuf)):
-            hop(piece(buf, 2 * seg, i), buf, kind, seg, i, h1_s, h1_r).wait_recv()
-        for part in reversed(range(NS)):
-            for kind, buf in ((0, kbuf), (1, vbuf)):
-                pass_on(kind, buf, i, part).start()
+    def landed(kind, buf, i):
+        hop(piece(buf, 2 * seg, i), buf, kind, seg, i, h1_s, h1_r).wait_recv()
+
+    def early(i, parts):
+        landed(1, vbuf, i)
+        for part in parts:
+            pass_on(1, vbuf, i, part).start()
+
+    def relay(i, parts):
+        landed(0, kbuf, i)
+
+        @pl.when(i // 2 != chip)
+        def _():
+            landed(1, vbuf, i)
+            for part in parts:
+                pass_on(0, kbuf, i, part).start()
+                pass_on(1, vbuf, i, part).start()
+
+        @pl.when(i // 2 == chip)
+        def _():
+            for part in parts:
+                pass_on(0, kbuf, i, part).start()
+
+    for i in (me, sib):
+        pl.when(i == 0)(functools.partial(early, i, final))
+        pl.when(i != 0)(functools.partial(early, i, usual))
+
+    def relay_usual(step, carry):
+        relay(nh - 1 - step, usual)
         return carry
 
-    lax.fori_loop(0, nh, relay, 0)
+    lax.fori_loop(0, nh - 1, relay_usual, 0)
+    relay(0, final)
     for jx, jc in arrival:
         source = partner(jx, jc)
         swap(2, qn, qseg, 0, source, source).wait_recv()
@@ -153,33 +178,36 @@
     col = lax.broadcasted_iota(jnp.int32, (t, 2 * seg), 1)
 
     def to_sibling(i, part, c):
-        at = (i, pl.ds(part * sub, sub), pl.ds(c * chunk, chunk))
+        slot, low, size = part
+        at = (i, pl.ds(low, size), pl.ds(c * chunk, chunk))
         return pltpu.make_async_remote_copy(
             src_ref=sib_out.at[at], dst_ref=sib_in.at[at],
-            send_sem=sib_s.at[i, part, c], recv_sem=sib_r.at[i, part, c],
+            send_sem=sib_s.at[i, slot, c], recv_sem=sib_r.at[i, slot, c],
             device_id={"head": sib},
         )
 
     def home(x, side, part, c):
+        slot, low, size = part
         columns = pl.ds(pl.multiple_of(side * half + c * chunk, DH), chunk)
-        return rbuf.at[x, pl.ds(part * sub, sub), columns]
+        return rbuf.at[x, pl.ds(low, size), columns]
 
     def to_owner(i, part, c, source, owner):
+        slot, low, size = part
         return pltpu.make_async_remote_copy(
-            src_ref=comb.at[i, pl.ds(part * sub, sub), pl.ds(c * chunk, chunk)],
+            src_ref=comb.at[i, pl.ds(low, size), pl.ds(c * chunk, chunk)],
             dst_ref=home(source // 2, source % 2, part, c),
-            send_sem=red_s.at[i, part, c], recv_sem=red_r.at[source, part, c],
+            send_sem=red_s.at[i, slot, c], recv_sem=red_r.at[source, slot, c],
             device_id={"head": owner},
         )
 
     def keep(i, part, c):
+        slot, low, size = part
         return pltpu.make_async_copy(
-            comb.at[i, pl.ds(part * sub, sub), pl.ds(c * chunk, chunk)],
-            home(chip, core, part, c), keep_sem.at[part, c],
-        )
-
-    def block(step, carry):
-        i = nh - 1 - step
+            comb.at[i, pl.ds(low, size), pl.ds(c * chunk, chunk)],
+            home(chip, core, part, c), keep_sem.at[slot, c],
+        )
+
+    def block(i, parts):
         rows = pl.ds(pl.multiple_of(i * t, t), t)
         keys = pl.ds(pl.multiple_of(i * t + t, t), 2 * seg)
         oldest = 2 * seg - first - i * t
@@ -199,10 +227,10 @@
                 p.astype(jnp.bfloat16), vbuf[keys, at], preferred_element_type=jnp.float32
             )
 
-        for part in reversed(range(NS)):
+        for part in parts:
             for kind, buf in ((0, kbuf), (1, vbuf)):
                 pass_on(kind, buf, i, part).wait_recv()
-            low = part * sub
+            slot, low, sub = part
             many = t - low
             keys = pl.ds(pl.multiple_of(i * t + low, sub), many)
             here = pl.ds(pl.multiple_of(i * t + low, sub), sub)
@@ -234,12 +262,9 @@
                 return jnp.dot(ho[spot, :], w_ref[:, at], preferred_element_type=jnp.float32)
 
             for c in range(NC):
-                sib_out[i, spot, pl.ds(c * chunk, chunk)] = project(1 - core, c).astype(
-                    jnp.bfloat16
-                )
+                at = pl.ds(c * chunk, chunk)
+                sib_out[i, spot, at] = project(1 - core, c).astype(jnp.bfloat16)
                 to_sibling(i, part, c).start()
-            for c in range(NC):
-                at = pl.ds(c * chunk, chunk)
                 mine = project(core, c)
                 to_sibling(i, part, c).wait_recv()
                 both = mine + sib_in[i, spot, at].astype(jnp.float32)
@@ -253,35 +278,56 @@
                 def _():
                     to_owner(i, part, c, me, i).start()
 
+    def block_usual(step, carry):
+        block(nh - 1 - step, usual)
         return carry
 
-    lax.fori_loop(0, nh, block, 0)
-
-    pieces = [(part, c) for part in reversed(range(NS)) for c in range(NC)]
-    for part, c in pieces:
-        keep(me, part, c).wait()
-        for jx, jc in arrival:
-            source = partner(jx, jc)
-            to_owner(source, part, c, source, source).wait_recv()
+    lax.fori_loop(0, nh - 1, block_usual, 0)
+    block(0, final)
+
+    def collect(parts):
+        for part in parts:
+            for c in range(NC):
+                keep(me, part, c).wait()
+                for jx, jc in arrival:
+                    source = partner(jx, jc)
+                    to_owner(source, part, c, source, source).wait_recv()
+
+    @pl.when(me == 0)
+    def _():
+        collect(final)
+
+    @pl.when(me != 0)
+    def _():
+        collect(usual)
 
     for jx, jc in arrival:
         peer = partner(jx, jc)
         swap(1, v_hbm, vbuf, 2 * seg, peer, me).wait_send()
         swap(0, kn, kbuf, 2 * seg, peer, me).wait_send()
         swap(2, qn, qseg, 0, peer, me).wait_send()
-        for part, c in pieces:
-            to_owner(peer, part, c, me, peer).wait_send()
-
-    def sent(i, carry):
+
+    def sent(i, parts):
         for kind, buf in ((0, kbuf), (1, vbuf)):
             hop(piece(buf, 2 * seg, i), buf, kind, seg, i, h1_s, h1_r).wait_send()
-            for part in range(NS):
+            for part in parts:
                 pass_on(kind, buf, i, part).wait_send()
-        for part, c in pieces:
-            to_sibling(i, part, c).wait_send()
+        for part in parts:
+            for c in range(NC):
+                to_sibling(i, part, c).wait_send()
+
+        @pl.when(me != i)
+        def _():
+            for part in parts:
+                for c in range(NC):
+                    to_owner(i, part, c, me, i).wait_send()
+
+    def sent_usual(step, carry):
+        sent(step + 1, usual)
         return carry
 
-    lax.fori_loop(0, nh, sent, 0)
+    lax.fori_loop(0, nh - 1, sent_usual, 0)
+    sent(0, final)
 
 
 def solution(mesh):
@@ -296,14 +342,14 @@
         half = width // 2
         bf16 = jnp.bfloat16
         dma = pltpu.SemaphoreType.DMA
-        anywhere = pl.BlockSpec(memory_space=pl.ANY)
+        anywhere = pl.BlockSpec(memory_space=pltpu.HBM)
         vmem = pl.BlockSpec(memory_space=pltpu.VMEM)
         parts = pl.pallas_call(
             functools.partial(kernel, nh, nb),
-            out_shape=jax.ShapeDtypeStruct((nh // 2, t, width), bf16),
+            out_shape=pltpu.VMEM((nh // 2, t, width), bf16),
             in_specs=[anywhere, anywhere, anywhere, vmem, anywhere,
                       pl.BlockSpec(memory_space=pltpu.SMEM)],
-            out_specs=anywhere,
+            out_specs=vmem,
             scratch_shapes=[
                 pltpu.VMEM((t, hd), bf16),
                 pltpu.VMEM((t, hd), bf16),
@@ -320,20 +366,20 @@
                 pltpu.VMEM((nh, t, half), bf16),
                 dma((3,)),
                 dma((3,)),
-                dma((NS, NC)),
+                dma((SLOTS, NC)),
                 dma((3, nh)),
                 dma((3, nh)),
                 dma((2, nh)),
                 dma((2, nh)),
-                dma((2, nh, NS)),
-                dma((2, nh, NS)),
-                dma((nh, NS, NC)),
-                dma((nh, NS, NC)),
-                dma((nh, NS, NC)),
-                dma((nh, NS, NC)),
+                dma((2, nh, SLOTS)),
+                dma((2, nh, SLOTS)),
+                dma((nh, SLOTS, NC)),
+                dma((nh, SLOTS, NC)),
+                dma((nh, SLOTS, NC)),
+                dma((nh, SLOTS, NC)),
             ],
             compiler_params=pltpu.CompilerParams(
-                collective_id=0, has_side_effects=True, vmem_limit_bytes=56 * 1024 * 1024
+                collective_id=0, has_side_effects=True, vmem_limit_bytes=54 * 1024 * 1024
             ),
         )(queries, keys, values, scale_qk.reshape(1, hd), w_out, stretch_start)
         return jnp.sum(parts.astype(jnp.float32), axis=0).astype(bf16)

time: 118 us -> 136 us (1.15)
  Pallas kernels: 114 us -> 134 us
  other arithmetic: 3.26 us -> 1.65 us
    pallas_call x1, Pallas kernels: 114 us -> 134 us  [shards(): pl.pallas_call(functools.partial(kernel, nh, nb), out_shape=pltpu.VMEM((n...]
    reduce_sum x1, other arithmetic: 3.26 us -> 1.65 us  [shards(): return jnp.sum(parts.astype(jnp.float32), axis=0).astype(bf16)]
where the time goes in v3:
time: 136 us
  Pallas kernels  134 us (99%)
  other arithmetic  1.65 us (1%)
    pallas_call x1, Pallas kernels, shards(): pl.pallas_call(functools.partial(kernel, nh, nb), out_shape=pltpu.VMEM((n...  134 us

profile of v3, /device:TPU:0, one launch (start us, length us, event | category | flops | bytes accessed | tf_op | source)
XLA Modules:
  0.0 136.2 jit_solution(12165813738406744819)
XLA Ops:
  0.7 133.9 %shard_map.64 = bf16[2,128,4096]{2,1,0:T(8,128)(2,1)S(1)} custom-call(bf16[128,4096]{1,0:T(8,128)(2,1)} %q_hbm.1, bf16[128,4096]{1,0:T(8,128)(2,1)} %k_hbm.1, bf16[128,4096]{1,0:T(8,128)(2,1)} %v_hbm.1, f32[1,4096]{1,0:T(1,128)} %bitcast.1, bf16[1024,4096]{1,0:T(8,128)(2,1)} %w_hbm.1, s32[1]{0:T(128)S(6)} %copy.7.start_ref), custom_call_target="tpu_custom_call" | custom-call | tf_op jit(solution)/shard_map/pallas_call | solution.py:347
  134.6 1.6 %reduce_sum.12 = bf16[128,4096]{1,0:T(8,128)(2,1)} reduce(bf16[2,128,4096]{2,1,0:T(8,128)(2,1)S(1)} %shard_map.64, bf16[]{:T(256)} %constant.2.clone.1), dimensions={0}, to_apply=%region_0.0 | reduce | flops 524288 | bytes 3145730 | tf_op jit(solution)/shard_map/reduce_sum | solution.py:385

commit v4 on v2

--- a/solution.py
+++ b/solution.py
@@ -296,14 +296,14 @@
         half = width // 2
         bf16 = jnp.bfloat16
         dma = pltpu.SemaphoreType.DMA
-        anywhere = pl.BlockSpec(memory_space=pl.ANY)
+        anywhere = pl.BlockSpec(memory_space=pltpu.HBM)
         vmem = pl.BlockSpec(memory_space=pltpu.VMEM)
         parts = pl.pallas_call(
             functools.partial(kernel, nh, nb),
-            out_shape=jax.ShapeDtypeStruct((nh // 2, t, width), bf16),
+            out_shape=pltpu.VMEM((nh // 2, t, width), bf16),
             in_specs=[anywhere, anywhere, anywhere, vmem, anywhere,
                       pl.BlockSpec(memory_space=pltpu.SMEM)],
-            out_specs=anywhere,
+            out_specs=vmem,
             scratch_shapes=[
                 pltpu.VMEM((t, hd), bf16),
                 pltpu.VMEM((t, hd), bf16),
@@ -333,7 +333,7 @@
                 dma((nh, NS, NC)),
             ],
             compiler_params=pltpu.CompilerParams(
-                collective_id=0, has_side_effects=True, vmem_limit_bytes=56 * 1024 * 1024
+                collective_id=0, has_side_effects=True, vmem_limit_bytes=54 * 1024 * 1024
             ),
         )(queries, keys, values, scale_qk.reshape(1, hd), w_out, stretch_start)
         return jnp.sum(parts.astype(jnp.float32), axis=0).astype(bf16)

time: 118 us -> 116 us (0.983)
  other arithmetic: 3.26 us -> 1.65 us
    reduce_sum x1, other arithmetic: 3.26 us -> 1.65 us  [shards(): return jnp.sum(parts.astype(jnp.float32), axis=0).astype(bf16)]
where the time goes in v4:
time: 116 us
  Pallas kernels  114 us (98%)
  other arithmetic  1.65 us (1%)
    pallas_call x1, Pallas kernels, shards(): pl.pallas_call(functools.partial(kernel, nh, nb), out_shape=pltpu.VMEM((n...  114 us

profile of v4, /device:TPU:0, one launch (start us, length us, event | category | flops | bytes accessed | tf_op | source)
XLA Modules:
  0.0 116.1 jit_solution(6974474626181357671)
XLA Ops:
  0.7 113.8 %shard_map.64 = bf16[2,128,4096]{2,1,0:T(8,128)(2,1)S(1)} custom-call(bf16[128,4096]{1,0:T(8,128)(2,1)} %q_hbm.1, bf16[128,4096]{1,0:T(8,128)(2,1)} %k_hbm.1, bf16[128,4096]{1,0:T(8,128)(2,1)} %v_hbm.1, f32[1,4096]{1,0:T(1,128)} %bitcast.1, bf16[1024,4096]{1,0:T(8,128)(2,1)} %w_hbm.1, s32[1]{0:T(128)S(6)} %copy.7.start_ref), custom_call_target="tpu_custom_call" | custom-call | tf_op jit(solution)/shard_map/pallas_call | solution.py:301
  114.5 1.6 %reduce_sum.12 = bf16[128,4096]{1,0:T(8,128)(2,1)} reduce(bf16[2,128,4096]{2,1,0:T(8,128)(2,1)S(1)} %shard_map.64, bf16[]{:T(256)} %constant.2.clone.1), dimensions={0}, to_apply=%region_0.0 | reduce | flops 524288 | bytes 3145730 | tf_op jit(solution)/shard_map/reduce_sum | solution.py:339
